TPU v7x, 128 devices: a whole 4x4x4 slice. The times are simulated.
128 devices in a mesh: view: 16 (over y, z), depth: 8 (over x, core).
Axes of the slice: x: 4, y: 4, z: 4, core: 2. Of those that a mesh axis runs over, the one named last changes fastest.
Arguments:
- features: bfloat16 [48, 1024, 32], P('view'), may hold values from -6 to 6
- view_lists: int32 [48, 10], P('view'), may hold values from 0 to 31
- requests: int32 [16, 16, 2], replicated, may hold values from 0 to 2
- warp_idx: int32 [48, 10, 64, 8, 128], P('view', None, None, 'depth'), may hold values from -682 to 1023
- conv_weight: bfloat16 [27, 8, 8], replicated, may hold values from -0.4375 to 0.4375
Outputs:
- regularized: bfloat16 [48, 8, 64, 8, 128], P('view', None, 'depth')
Inputs may be any that keep to these rules, and one draw needn't show every extreme that they name: `warp_idx`: A negative entry marks a sample that falls outside the source tile and is left out of the sum and the count.
All inputs are finite; a program needn't handle non-finite values.
Results may differ from a plain program's by a relative error of at most 0.0049.
Values may be sent and summed in bfloat16 or wider, within the bound.
No kernel may reach another device: no remote copies, remote signals or barrier semaphores. Data moves between devices by JAX's collectives and lax.ppermute only.
A program may use at most 128 MiB of HBM per device.

v0:
```python
import jax
import jax.numpy as jnp
from jax import lax
from jax.sharding import PartitionSpec as P


def padded_2(cells, sides, width):
    for axis, dim in sides:
        count = lax.axis_size(axis)
        ends = count - 1
        head = lax.slice_in_dim(cells, 0, width, axis=dim)
        tail = lax.slice_in_dim(cells, cells.shape[dim] - width, cells.shape[dim], axis=dim)
        cells = jnp.concatenate(
            [
                lax.ppermute(tail, axis, [(i, (i + 1) % count) for i in range(ends)]),
                cells,
                lax.ppermute(head, axis, [((i + 1) % count, i) for i in range(ends)]),
            ],
            axis=dim,
        )
    return cells


def mix_taps(padded, conv_weight, depth_out, rows_out, cols_out):
    summed = None
    for depth_tap in range(3):
        for row_tap in range(3):
            for col_tap in range(3):
                shifted = padded[
                    :,
                    :,
                    depth_tap : depth_tap + depth_out,
                    row_tap : row_tap + rows_out,
                    col_tap : col_tap + cols_out,
                ]
                kernel = conv_weight[9 * depth_tap + 3 * row_tap + col_tap]
                term = jnp.einsum(
                    "vgdhw,gk->vkdhw", shifted, kernel, preferred_element_type=jnp.float32
                )
                summed = term if summed is None else summed + term
    return summed


def on_device(features, view_lists, requests, warp_idx, conv_weight):
    view_here = lax.axis_index("view")
    depth_here = lax.axis_index("depth")
    depth_count = lax.axis_size("depth")
    local_views = features.shape[0]
    pixels = features.shape[1]
    channels = features.shape[2]
    sources = warp_idx.shape[1]
    planes = warp_idx.shape[2]
    row_count = warp_idx.shape[3]
    columns = warp_idx.shape[4]
    groups = conv_weight.shape[1]
    asked = requests.shape[2]
    tile_pool = lax.all_gather(features, "view", axis=0, tiled=True)
    owner_dev = view_lists // asked
    slot_index = view_lists % asked
    source_ids = owner_dev * local_views + requests[view_here, owner_dev, slot_index]
    flat_pool = tile_pool.reshape(-1, channels)
    own_pixels = row_count * columns
    own_rows = lax.dynamic_slice_in_dim(features, depth_here * own_pixels, own_pixels, 1)

    def one_view(item):
        own_tile, warp_rows, view_sources = item
        usable = (warp_rows >= 0).reshape(sources, planes, own_pixels)
        picks = view_sources[:, None, None, None] * pixels + jnp.maximum(warp_rows, 0)
        warped = jnp.take(flat_pool, picks.reshape(-1), axis=0)
        warped = warped.reshape(sources, planes, own_pixels, groups, channels // groups)
        own_groups = own_tile.reshape(own_pixels, groups, channels // groups)
        products = jnp.einsum(
            "sdpgk,pgk->sdpg", warped, own_groups, preferred_element_type=jnp.float32
        )
        masked = jnp.where(usable[..., None], products, jnp.float32(0.0))
        live_count = jnp.sum(usable.astype(jnp.float32), axis=0)
        corr = 0.5 * jnp.sum(masked, axis=0) / jnp.maximum(live_count, jnp.float32(1.0))[..., None]
        corr = jnp.transpose(corr, (2, 0, 1)).reshape(groups, planes, row_count, columns)
        return corr.astype(jnp.bfloat16)

    cost_rows = lax.map(one_view, (own_rows, warp_idx, source_ids))
    slab_planes = planes // depth_count
    slab = lax.all_to_all(cost_rows, "depth", split_axis=2, concat_axis=3, tiled=True)
    rimmed = padded_2(slab, (("depth", 2),), 1)
    rimmed = jnp.pad(rimmed, ((0, 0), (0, 0), (0, 0), (1, 1), (1, 1)))
    summed = mix_taps(rimmed, conv_weight, slab_planes, row_count * depth_count, columns)
    return summed.astype(jnp.bfloat16)


def solution(mesh):
    return jax.shard_map(
        on_device,
        mesh=mesh,
        in_specs=(
            P("view", None, None),
            P("view", None),
            P(),
            P("view", None, None, "depth", None),
            P(),
        ),
        out_specs=P("view", None, "depth", None, None),
        check_vma=False,
    )
```

profile of v0, /device:TPU:1, one launch (start us, length us, event | category | flops | bytes accessed | tf_op | source)
XLA Modules:
  0.0 1019.4 jit_solution(8187742426238221678)
XLA Ops:
  8.1 0.9 gather_fusion.1
  9.1 0.8 constant_dynamic-slice_fusion.2
  9.9 50.2 %all-gather.2.cloned.1.call-done = bf16[48,1024,32]{1,2,0:T(8,128)(2,1)} async-done(((bf16[3,1024,32]{1,2,0:T(8,128)(2,1)}), bf16[48,1024,32]{1,2,0:T(8,128)(2,1)}) %all-gather.2.cloned.1.call-update) | async-done | bytes 3145744 | tf_op jit(solution)/shard_map/all_gather | solution.py:57
  60.1 11.0 %copy.343 = bf16[48,1024,32]{2,1,0:T(8,128)(2,1)} copy(bf16[48,1024,32]{1,2,0:T(8,128)(2,1)} %all-gather.2.cloned.1.call-done) | data formatting | bytes 6291456 | tf_op jit(solution)/shard_map/while | solution.py:81
  71.1 909.2 %while.10 = (s32[]{:T(128)}, bf16[3,8,64,1,128]{4,1,0,3,2:T(8,128)(2,1)}, s32[3,10,64,1,128]{4,2,1,3,0:T(8,128)S(1)}, bf16[3,128,32]{1,2,0:T(8,128)(2,1)S(1)}, s...) while((s32[]{:T(128)}, bf16[3,8,64,1,128]{4,1,0,3,2:T(8,128)(2,1)}, ...), condition=%wide.region_3.4_spmd, body=%wide.region_0.3_spmd.sunk | while | flops 12587020 | bytes 46916348 | solution.py:81
  72.0 278.2 %gather_fusion = bf16[81920,32]{1,0:T(8,128)(2,1)} fusion(bf16[49152,32]{1,0:T(8,128)(2,1)} %get-tuple-element.177, s32[81920]{0:T(1024)S(1)} %broadcast_clamp_fusion.2), kind=kCustom, calls=%fused_computation.clone.1 | custom fusion | bytes 10813440 | tf_op jit(solution)/shard_map/while/body/eval_jaxpr/jit(_take)/gather | solution.py:69
  350.2 17.3 %copy.427 = bf16[81920,32]{0,1:T(8,128)(2,1)} copy(bf16[81920,32]{1,0:T(8,128)(2,1)} %gather_fusion) | data formatting | bytes 10485760 | tf_op jit(solution)/shard_map/while/body/eval_jaxpr/jit(_take)/gather | solution.py:69
  367.5 3.7 copy.428
  371.2 1.6 multiply_reduce_fusion.2
  373.5 0.8 copy_dynamic-update-slice_fusion.2
  375.0 278.2 %gather_fusion = bf16[81920,32]{1,0:T(8,128)(2,1)} fusion(bf16[49152,32]{1,0:T(8,128)(2,1)} %get-tuple-element.177, s32[81920]{0:T(1024)S(1)} %broadcast_clamp_fusion.2), kind=kCustom, calls=%fused_computation.clone.1 | custom fusion | bytes 10813440 | tf_op jit(solution)/shard_map/while/body/eval_jaxpr/jit(_take)/gather | solution.py:69
  653.2 17.3 %copy.427 = bf16[81920,32]{0,1:T(8,128)(2,1)} copy(bf16[81920,32]{1,0:T(8,128)(2,1)} %gather_fusion) | data formatting | bytes 10485760 | tf_op jit(solution)/shard_map/while/body/eval_jaxpr/jit(_take)/gather | solution.py:69
  670.5 3.7 copy.428
  674.3 1.6 multiply_reduce_fusion.2
  678.1 278.2 %gather_fusion = bf16[81920,32]{1,0:T(8,128)(2,1)} fusion(bf16[49152,32]{1,0:T(8,128)(2,1)} %get-tuple-element.177, s32[81920]{0:T(1024)S(1)} %broadcast_clamp_fusion.2), kind=kCustom, calls=%fused_computation.clone.1 | custom fusion | bytes 10813440 | tf_op jit(solution)/shard_map/while/body/eval_jaxpr/jit(_take)/gather | solution.py:69
  956.3 17.3 %copy.427 = bf16[81920,32]{0,1:T(8,128)(2,1)} copy(bf16[81920,32]{1,0:T(8,128)(2,1)} %gather_fusion) | data formatting | bytes 10485760 | tf_op jit(solution)/shard_map/while/body/eval_jaxpr/jit(_take)/gather | solution.py:69
  973.6 3.7 copy.428
  977.4 1.6 multiply_reduce_fusion.2
  980.3 5.5 all-to-all-start
  989.8 3.8 all-to-all-done
  993.7 3.3 collective-permute-start
  997.0 2.1 collective-permute-start.1
  999.4 3.0 collective-permute-done.1
  1011.7 0.8 copy.309
  (115 shorter events, 20.7 us)
Async XLA Ops:
  6.5 1.5 copy-start
  6.5 3.3 copy-start.4
  6.5 53.6 %all-gather.2.cloned.1.call-start = ((), (), s32[]{:S(2)}) async-start(), calls=%async_computation.1 | async-start | bytes 3342336 | tf_op jit(solution)/shard_map/all_gather | solution.py:57
  9.8 61.3 %copy-start.3 = (s32[3,10,64,1,128]{4,3,2,1,0:T(1,128)S(1)}, s32[3,10,64,1,128]{4,3,2,1,0:T(1,128)}, u32[]{:S(2)}) copy-start(s32[3,10,64,1,128]{4,3,2,1,0:T(1,128)} %param.10) | copy-start | bytes 2949124
  71.1 914.7 %copy-start.2 = (bf16[27,8,8]{0,2,1:T(8,128)(2,1)S(1)}, bf16[27,8,8]{0,2,1:T(8,128)(2,1)}, u32[]{:S(2)}) copy-start(bf16[27,8,8]{0,2,1:T(8,128)(2,1)} %param.11) | copy-start | bytes 10372
  980.3 13.2 %all-to-all-start = ((bf16[3,8,64,1,128]{4,1,0,3,2:T(8,128)(2,1)}), bf16[3,8,64,1,128]{4,1,0,3,2:T(8,128)(2,1)S(1)}, u32[]{:S(2)}, u32[]{:S(2)}) async-start(bf16[3,8,64,1,128]{4,1,0,3,2:T(8,128)(2,1)} %get-tuple-element.37), calls=%async_computation | async-start | bytes 786432 | tf_op jit(solution)/shard_map/all_to_all | solution.py:83
  993.7 5.7 collective-permute-start
  997.0 5.4 collective-permute-start.1
  1011.0 1.5 copy-start.1
Sparse Core Ops, SparseCore 0:
  9.5 50.5 all-gather.1
where the time goes:
time: 1020 us
  local copies, waits for them, and re-layouts  918 us (90%)
  waiting for transfers between devices  57.7 us (6%)
  between operations  13.7 us (1%)
  starting transfers between devices  10.9 us (1%)
    gather x6, local copies, waits for them, and re-layouts, one_view(): warped = jnp.take(flat_pool, picks.reshape(-1), axis=0)  887 us
    all_gather x1, waiting for transfers between devices, on_device(): tile_pool = lax.all_gather(features, 'view', axis=0, tiled=True)  50.2 us
  transfers between devices with their start and end apart: 4, of which 3 were waited for; matrix products, arithmetic and copies ran while one was open for 1% of the time, Pallas kernels for 0%

commit v1 on v0

--- a/solution.py
+++ b/solution.py
@@ -54,7 +54,15 @@
     columns = warp_idx.shape[4]
     groups = conv_weight.shape[1]
     asked = requests.shape[2]
-    tile_pool = lax.all_gather(features, "view", axis=0, tiled=True)
+    tile_pool = jnp.concatenate(
+        jax.lax.all_to_all(
+            jnp.stack([features for _ in range(jax.lax.axis_size("view"))], 0),
+            axis_name="view",
+            split_axis=0,
+            concat_axis=0,
+        ),
+        0,
+    )
     owner_dev = view_lists // asked
     slot_index = view_lists % asked
     source_ids = owner_dev * local_views + requests[view_here, owner_dev, slot_index]

time: 1020 us -> 1010 us (level)
  between operations: 13.7 us -> 0.28 us
  waiting for transfers between devices: 57.7 us -> 45.2 us
  starting transfers between devices: 10.9 us -> 21.4 us
    all_gather x1 -> x0, waiting for transfers between devices: 50.2 us -> none  [on_device(): tile_pool = lax.all_gather(features, 'view', axis=0, tiled=True)]
    all_to_all x0 -> x1, waiting for transfers between devices: none -> 38.4 us  [on_device(): jax.lax.all_to_all(jnp.stack([features for _ in range(jax.lax.axis_size('...]
where the time goes in v1:
time: 1010 us
  local copies, waits for them, and re-layouts  918 us (91%)
  waiting for transfers between devices  45.2 us (4%)
  starting transfers between devices  21.4 us (2%)
  other arithmetic  15 us (1%)
    gather x6, local copies, waits for them, and re-layouts, one_view(): warped = jnp.take(flat_pool, picks.reshape(-1), axis=0)  886 us
    all_to_all x1, waiting for transfers between devices, on_device(): jax.lax.all_to_all(jnp.stack([features for _ in range(jax.lax.axis_size('...  38.4 us
  transfers between devices with their start and end apart: 4, of which 3 were waited for; matrix products, arithmetic and copies ran while one was open for 1% of the time, Pallas kernels for 0%

profile of v1, /device:TPU:1, one launch (start us, length us, event | category | flops | bytes accessed | tf_op | source)
XLA Modules:
  0.0 1009.3 jit_solution(6272334789385146489)
XLA Ops:
  0.0 3.0 stack.2
  3.0 8.7 all-to-all-start
  13.6 38.4 %all-to-all-done = bf16[16,3,1024,32]{2,3,1,0:T(8,128)(2,1)S(1)} async-done(((bf16[16,3,1024,32]{2,3,1,0:T(8,128)(2,1)}), bf16[16,3,1024,32]{2,3,1,0:T(8,128)(2,1)S(1)}, u32[]{:S(2)}, u32[]{:S(2)}) %all-to-all-start) | async-done | bytes 3145760 | tf_op jit(solution)/shard_map/all_to_all | solution.py:58
  52.1 8.6 copy.343
  60.6 914.7 %while.10 = (s32[]{:T(128)}, bf16[3,8,64,1,128]{4,1,0,3,2:T(8,128)(2,1)}, s32[3,10,64,1,128]{4,2,1,3,0:T(8,128)}, bf16[3,128,32]{1,2,0:T(8,128)(2,1)S(1)}, s32[3...) while((s32[]{:T(128)}, bf16[3,8,64,1,128]{4,1,0,3,2:T(8,128)(2,1)}, ...), condition=%wide.region_3.4_spmd, body=%wide.region_0.3_spmd.sunk | while | flops 12587020 | bytes 46916348 | solution.py:89
  60.6 1.2 compare_and_fusion.2
  62.4 278.1 %gather_fusion = bf16[81920,32]{1,0:T(8,128)(2,1)} fusion(bf16[49152,32]{1,0:T(8,128)(2,1)} %get-tuple-element.177, s32[81920]{0:T(1024)S(1)} %broadcast_clamp_fusion.2), kind=kCustom, calls=%fused_computation.clone.1 | custom fusion | bytes 10813440 | tf_op jit(solution)/shard_map/while/body/eval_jaxpr/jit(_take)/gather | solution.py:77
  340.5 17.3 %copy.427 = bf16[81920,32]{0,1:T(8,128)(2,1)} copy(bf16[81920,32]{1,0:T(8,128)(2,1)} %gather_fusion) | data formatting | bytes 10485760 | tf_op jit(solution)/shard_map/while/body/eval_jaxpr/jit(_take)/gather | solution.py:77
  357.8 3.7 copy.428
  361.6 1.6 multiply_reduce_fusion.2
  365.5 1.2 compare_and_fusion.2
  367.3 278.1 %gather_fusion = bf16[81920,32]{1,0:T(8,128)(2,1)} fusion(bf16[49152,32]{1,0:T(8,128)(2,1)} %get-tuple-element.177, s32[81920]{0:T(1024)S(1)} %broadcast_clamp_fusion.2), kind=kCustom, calls=%fused_computation.clone.1 | custom fusion | bytes 10813440 | tf_op jit(solution)/shard_map/while/body/eval_jaxpr/jit(_take)/gather | solution.py:77
  645.4 17.3 %copy.427 = bf16[81920,32]{0,1:T(8,128)(2,1)} copy(bf16[81920,32]{1,0:T(8,128)(2,1)} %gather_fusion) | data formatting | bytes 10485760 | tf_op jit(solution)/shard_map/while/body/eval_jaxpr/jit(_take)/gather | solution.py:77
  662.7 3.7 copy.428
  666.5 1.6 multiply_reduce_fusion.2
  672.2 278.1 %gather_fusion = bf16[81920,32]{1,0:T(8,128)(2,1)} fusion(bf16[49152,32]{1,0:T(8,128)(2,1)} %get-tuple-element.177, s32[81920]{0:T(1024)S(1)} %broadcast_clamp_fusion.2), kind=kCustom, calls=%fused_computation.clone.1 | custom fusion | bytes 10813440 | tf_op jit(solution)/shard_map/while/body/eval_jaxpr/jit(_take)/gather | solution.py:77
  950.3 17.3 %copy.427 = bf16[81920,32]{0,1:T(8,128)(2,1)} copy(bf16[81920,32]{1,0:T(8,128)(2,1)} %gather_fusion) | data formatting | bytes 10485760 | tf_op jit(solution)/shard_map/while/body/eval_jaxpr/jit(_take)/gather | solution.py:77
  967.6 3.7 copy.428
  971.4 1.6 multiply_reduce_fusion.2
  975.3 7.3 all-to-all-start.1
  986.5 3.8 all-to-all-done.1
  990.5 3.3 collective-permute-start
  993.8 2.1 collective-permute-start.1
  996.2 3.0 collective-permute-done.1
  (113 shorter events, 26.1 us)
Async XLA Ops:
  0.0 11.8 %copy-start = (s32[16,16,2]{1,2,0:T(2,128)S(1)}, s32[16,16,2]{1,2,0:T(2,128)}, u32[]{:S(2)}) copy-start(s32[16,16,2]{1,2,0:T(2,128)} %param.9) | copy-start | bytes 6148
  3.0 8.7 copy-start.3
  3.0 49.1 %all-to-all-start = ((bf16[16,3,1024,32]{2,3,1,0:T(8,128)(2,1)}), bf16[16,3,1024,32]{2,3,1,0:T(8,128)(2,1)S(1)}, u32[]{:S(2)}, u32[]{:S(2)}) async-start(bf16[16,3,1024,32]{2,3,1,0:T(8,128)(2,1)} %stack.2), calls=%async_computation | async-start | bytes 6291456 | tf_op jit(solution)/shard_map/all_to_all | solution.py:58
  60.6 922.0 %copy-start.2 = (bf16[27,8,8]{0,2,1:T(8,128)(2,1)S(1)}, bf16[27,8,8]{0,2,1:T(8,128)(2,1)}, u32[]{:S(2)}) copy-start(bf16[27,8,8]{0,2,1:T(8,128)(2,1)} %param.11) | copy-start | bytes 10372
  975.3 15.0 %all-to-all-start.1 = ((bf16[3,8,64,1,128]{4,1,0,3,2:T(8,128)(2,1)}), bf16[3,8,64,1,128]{4,1,0,3,2:T(8,128)(2,1)S(1)}, u32[]{:S(2)}, u32[]{:S(2)}) async-start(bf16[3,8,64,1,128]{4,1,0,3,2:T(8,128)(2,1)} %get-tuple-element.37), calls=%async_computation.1 | async-start | bytes 786432 | tf_op jit(solution)/shard_map/all_to_all | solution.py:91
  990.5 5.7 collective-permute-start
  993.8 5.4 collective-permute-start.1
  1007.8 1.5 copy-start.1
